TPU v7x, 32 devices: a whole 2x2x4 slice. The times are simulated.
32 devices in a mesh: seq: 8 (over z, x), head: 4 (over y, core).
Axes of the slice: x: 2, y: 2, z: 4, core: 2. Of those that a mesh axis runs over, the one named last changes fastest.
Arguments:
- queries: bfloat16 [1024, 4096], P('seq', 'head'), may hold values from -250 to 250
- key_vectors: bfloat16 [1024, 512], P('seq', 'head'), may hold values from -250 to 250
- value_vectors: bfloat16 [1024, 512], P('seq', 'head'), may hold values from -20 to 20
- positions: int32 [1024], P('seq'), may hold values from 0 to 511, as said below
- query_map: float32 [32, 128, 128], P('head'), may hold values from -0.5 to 0.5
- key_map: float32 [4, 128, 128], P('head'), may hold values from -0.5 to 0.5
Outputs:
- grad_queries: float32 [1024, 4096], P('seq', 'head')
- grad_keys: float32 [1024, 512], P('seq', 'head')
- grad_values: float32 [1024, 512], P('seq', 'head')
- query_map_grad: float32 [32, 128, 128], P('head')
- key_map_grad: float32 [4, 128, 128], P('head')
Inputs may be any that keep to these rules, and one draw needn't show every extreme that they name: positions[0] is 0, and each later position is either 0 (a document begins) or one more than the position before it; the slab holds at most 4 documents, and one of them is exactly 512 tokens long.
All inputs are finite; a program needn't handle non-finite values.
Results may differ from a plain program's by a relative error of at most 0.0025.
Values may be sent and summed in bfloat16 or wider, within the bound.
A program may use at most 64 MiB of HBM per device.

v0:
```python
import functools
import math

import jax
import jax.numpy as jnp
from jax import lax
from jax.experimental import pallas as pl
from jax.experimental.pallas import tpu as pltpu
from jax.sharding import PartitionSpec as P

F32 = jnp.float32
BF16 = jnp.bfloat16
NEGATIVE = -1e30
EPSILON = 1e-06
GRANT = 66_000_000
MESH = pl.DeviceIdType.MESH

NN = (((1,), (0,)), ((), ()))
NT = (((1,), (1,)), ((), ()))
TN = (((0,), (0,)), ((), ()))


def split(value):
    high = value.astype(BF16)
    low = (value - high.astype(F32)).astype(BF16)
    return (high, low)


def single(value):
    return (value.astype(BF16),)


def product(left, right, dims):
    total = lax.dot_general(left[0], right[0], dims, preferred_element_type=F32)
    if len(left) > 1:
        total = total + lax.dot_general(left[1], right[0], dims, preferred_element_type=F32)
    if len(right) > 1:
        total = total + lax.dot_general(left[0], right[1], dims, preferred_element_type=F32)
    return total


def softmax_pair(logits):
    up = jnp.exp(logits - jnp.max(logits, axis=-1, keepdims=True))
    low = jnp.exp(jnp.min(logits, axis=-1, keepdims=True) - logits)
    up = up / jnp.sum(up, axis=-1, keepdims=True)
    low = low / jnp.sum(low, axis=-1, keepdims=True)
    return jnp.concatenate([up, low], axis=-1)


def feature_back(phi, grad_phi, half):
    product_ = phi * grad_phi
    up, low = (product_[:, :half], product_[:, half:])
    up = up - phi[:, :half] * jnp.sum(up, axis=-1, keepdims=True)
    low = low - phi[:, half:] * jnp.sum(low, axis=-1, keepdims=True)
    return up - low


def kernel(
    count, heads, reach, batch, q_hbm, k_hbm, v_hbm, pos_hbm, qmap_hbm, kmap_hbm,
    gq_hbm, gk_hbm, gv_hbm, gqm_hbm, gkm_hbm,
    q_ref, pos_ref, qmap_ref, kmap_ref, load_s,
    gq_ref, gk_ref, gv_ref, gqm_ref, gkm_ref, store_s,
    win_k, win_v, bias, phi, inner_s, gn_s, gd_s, dlog_s, back_s, back_send, back_recv,
    q_loc, q_recv, q_all, q_own, k_loc, k_recv, k_all, norm_all,
    k_ss, k_rs, v_ss, v_rs, b_ss, b_rs, r_ss, r_rs, a_ss, a_rs, m_ss, m_rs, n_ss, n_rs, h_ss, h_rs,
):
    me = lax.axis_index("seq")
    my_head = lax.axis_index("head")
    rows, dim = k_hbm.shape
    group, _, half = qmap_ref.shape
    feat = 2 * half
    per_head = count // group
    shard = dim // per_head
    span = batch * rows
    scaling = 1.0 / math.sqrt(dim)
    k_shard = k_loc.shape[1]
    owners = k_loc.shape[0]
    k_ref = win_k.at[pl.ds(reach * rows, rows)]
    v_ref = win_v.at[pl.ds(reach * rows, rows)]
    loads = [
        pltpu.make_async_copy(src, dst, load_s.at[i])
        for i, (src, dst) in enumerate(
            ((k_hbm, k_ref), (v_hbm, v_ref), (pos_hbm, pos_ref), (kmap_hbm, kmap_ref), (q_hbm, q_ref), (qmap_hbm, qmap_ref))
        )
    ]
    for load in loads:
        load.start()
    stores = [
        pltpu.make_async_copy(src, dst, store_s.at[i])
        for i, (src, dst) in enumerate(
            ((gq_ref, gq_hbm), (gk_ref, gk_hbm), (gv_ref, gv_hbm), (gqm_ref, gqm_hbm), (gkm_ref, gkm_hbm))
        )
    ]

    def remote(src, dst, send, recv, **where):
        return pltpu.make_async_remote_copy(
            src_ref=src, dst_ref=dst, send_sem=send, recv_sem=recv,
            device_id=where, device_id_type=MESH,
        )

    barrier = pltpu.get_barrier_semaphore()
    for step in range(1, count):
        pl.semaphore_signal(
            barrier, inc=1, device_id={"seq": lax.rem(me + step, count)}, device_id_type=MESH
        )
    for step in range(1, heads):
        pl.semaphore_signal(
            barrier, inc=1, device_id={"head": lax.rem(my_head + step, heads)}, device_id_type=MESH
        )
    loads[0].wait()
    loads[1].wait()
    pl.semaphore_wait(barrier, count + heads - 2)

    def block_copies(step):
        place = pl.ds((reach - step) * rows, rows)
        return (
            remote(k_ref, win_k.at[place], k_ss.at[step - 1], k_rs.at[step - 1], seq=lax.rem(me + step, count)),
            remote(v_ref, win_v.at[place], v_ss.at[step - 1], v_rs.at[step - 1], seq=lax.rem(me + step, count)),
        )

    for step in range(1, reach + 1):
        @pl.when(me + step < count)
        def _():
            for copy in block_copies(step):
                copy.start()

        @pl.when(me < step)
        def _():
            place = pl.ds((reach - step) * rows, rows)
            win_k[place, :] = jnp.zeros((rows, dim), BF16)
            win_v[place, :] = jnp.zeros((rows, dim), BF16)

    loads[2].wait()
    loads[3].wait()

    row_base = me * rows
    token = row_base + lax.broadcasted_iota(jnp.int32, (rows, rows), 0)
    positions = jnp.broadcast_to(pos_ref[...].astype(F32), (rows, rows)).T.astype(jnp.int32)
    starts = token - positions
    lane = lax.broadcasted_iota(jnp.int32, (rows, rows), 1)
    for slot in range(reach + 1):
        key_index = (me - reach + slot) * rows + lane
        seen = (key_index <= token) & (key_index >= starts)
        bias[:, slot * rows : (slot + 1) * rows] = jnp.where(seen, 0.0, NEGATIVE)
    own = jnp.where((row_base + lane <= token) & (row_base + lane >= starts), 1.0, 0.0)
    crossing = jnp.where(starts < row_base, 1.0, 0.0)[:, :1]
    keeping = jnp.where(starts == starts[rows - 1 :, :], 1.0, 0.0)[:, :1]
    first_start = starts[:1, :1]
    last_start = starts[rows - 1 :, :1]

    kmap = split(kmap_ref[0])
    key_phi = softmax_pair(product((k_ref[...],), kmap, NN))
    key_parts = split(key_phi)

    def features(turn, carry):
        for h in range(batch):
            g = turn * batch + h
            q = q_ref[:, pl.ds(pl.multiple_of(g * dim, dim), dim)]
            place = pl.ds(pl.multiple_of(g * rows, rows), rows)
            phi[place, :] = softmax_pair(product((q,), split(qmap_ref[g]), NN))
        return carry

    loads[4].wait()
    loads[5].wait()
    lax.fori_loop(0, group // batch, features, 0)

    for step in range(1, reach + 1):
        @pl.when(me >= step)
        def _():
            for copy in block_copies(step):
                copy.wait_recv()

    earlier = win_k[: reach * rows, :]
    past_phi = softmax_pair(product((earlier,), kmap, NN))
    past_index = (me - reach) * rows + lax.broadcasted_iota(jnp.int32, (reach * rows, 1), 0)
    past_phi = past_phi * jnp.where(past_index >= first_start, 1.0, 0.0)
    state = product(split(past_phi), (win_v[: reach * rows, :],), TN)
    norms = jnp.sum(past_phi, axis=0, keepdims=True)
    state_parts = split(state)
    value = (v_ref[...],)

    back_s[...] = jnp.zeros_like(back_s)

    def stacked(part):
        return jnp.broadcast_to(part[None], (batch,) + part.shape).reshape(
            (batch * part.shape[0],) + part.shape[1:]
        )

    def forward(turn):
        place = pl.ds(pl.multiple_of(turn * span, span), span)
        q = jnp.concatenate(
            [
                q_ref[:, pl.ds(pl.multiple_of((turn * batch + h) * dim, dim), dim)]
                for h in range(batch)
            ],
            axis=0,
        )
        scores = lax.dot_general(q, win_k[...], NT, preferred_element_type=F32) * scaling
        scores = (scores.reshape(batch, rows, -1) + bias[...][None]).reshape(span, -1)
        weights = jnp.exp(scores - jnp.max(scores, axis=-1, keepdims=True))
        total = jnp.sum(weights, axis=-1, keepdims=True)
        teacher = lax.dot_general(weights.astype(BF16), win_v[...], NN, preferred_element_type=F32)
        teacher = teacher / total
        q_phi = phi[place, :]
        cross = stacked(crossing)
        crossed = q_phi * cross
        inner = product(split(q_phi), key_parts, NT) * stacked(own)
        crossed_parts = split(crossed)
        numer = product(split(inner), value, NN) + product(crossed_parts, state_parts, NN)
        denom = jnp.sum(inner, axis=-1, keepdims=True) + jnp.sum(
            crossed * norms, axis=-1, keepdims=True
        )
        student = numer / denom
        error = student - teacher
        grad_numer = error / denom
        grad_denom = -jnp.sum(error * student, axis=-1, keepdims=True) / denom
        inner_s[place, :] = inner
        gn_s[place, :] = grad_numer
        gd_s[place, :] = jnp.broadcast_to(grad_denom, (span, dim))
        back_s[:feat, :] += product(crossed_parts, split(grad_numer), TN)
        down = jnp.sum(crossed * grad_denom, axis=0, keepdims=True)
        back_s[feat : feat + 1, :] += down[:, :half]
        back_s[feat + 1 : feat + 2, :] += down[:, half:]

    def shard_copy(target):
        return remote(q_loc.at[target], q_recv.at[me], r_ss.at[target], r_rs.at[me], seq=target)

    def backward(turn, carry):
        grad_kphi, grad_values = carry
        place = pl.ds(pl.multiple_of(turn * span, span), span)
        q_phi = phi[place, :]
        grad_numer = split(gn_s[place, :])
        grad_denom = gd_s[place, :1]
        mixing = (product(grad_numer, value, NT) + grad_denom) * stacked(own)
        mixing = split(mixing)
        grad_qphi = product(mixing, key_parts, NN)
        grad_qphi = grad_qphi + stacked(crossing) * (
            product(grad_numer, state_parts, NT) + grad_denom * norms
        )
        dlog = feature_back(q_phi, grad_qphi, half)
        dlog_s[place, :] = dlog
        for h in range(batch):
            g = turn * batch + h
            q = q_ref[:, pl.ds(pl.multiple_of(g * dim, dim), dim)]
            grad_map = product((q,), split(dlog[h * rows : (h + 1) * rows]), TN)
            for part in range(per_head):
                target = g * per_head + part
                piece = grad_map[part * shard : (part + 1) * shard]
                q_loc[target] = piece.astype(BF16)

                @pl.when(target == me)
                def _():
                    q_own[...] = piece

                @pl.when(target != me)
                def _():
                    shard_copy(target).start()

        grad_kphi = grad_kphi + product(mixing, split(q_phi), TN)
        grad_values = grad_values + product(split(inner_s[place, :]), grad_numer, TN)
        return (grad_kphi, grad_values)

    def back_copy(step):
        return remote(
            back_send, back_recv.at[step - 1], b_ss.at[step - 1], b_rs.at[step - 1],
            seq=lax.rem(me + count - step, count),
        )

    sums = (jnp.zeros((rows, feat), F32), jnp.zeros((rows, dim), F32))
    for turn in range(group // batch):
        forward(turn)
        if turn == group // batch - 1:
            origin = jnp.floor(first_start.astype(F32) * (1.0 / rows))
            back_s[feat + 8 :, :] = jnp.broadcast_to(origin, (back_s.shape[0] - feat - 8, dim))
            back_send[...] = back_s[...].astype(BF16)

            for step in range(1, reach + 1):
                @pl.when(me >= step)
                def _():
                    back_copy(step).start()

        sums = backward(turn, sums)
    grad_kphi, grad_values = sums

    for step in range(1, reach + 1):
        @pl.when(me + step < count)
        def _():
            back_copy(step).wait_recv()

        @pl.when(me + step >= count)
        def _():
            back_recv[step - 1] = jnp.full(back_recv.shape[1:], 2.0 * count, BF16)

    mine = me.astype(F32)
    back = jnp.zeros((feat + 8, dim), F32)
    for step in range(1, reach + 1):
        arrived = back_recv[step - 1].astype(F32)
        back = back + jnp.where(arrived[feat + 8 : feat + 9, :1] <= mine, arrived[: feat + 8], 0.0)
    back_norms = jnp.concatenate([back[feat : feat + 1], back[feat + 1 : feat + 2]], axis=1)
    back_parts = single(back[:feat])
    grad_kphi = grad_kphi + keeping * (product(value, back_parts, NT) + back_norms)
    gv_ref[...] = grad_values + keeping * product(key_parts, back_parts, NN)
    key_dlog = split(feature_back(key_phi, grad_kphi, half))
    key_grad = product((k_ref[...],), key_dlog, TN)
    for owner in range(owners):
        k_loc[owner] = key_grad[owner * k_shard : (owner + 1) * k_shard]

    def key_copy(target):
        return remote(k_loc.at[target], k_recv.at[me], n_ss.at[target], n_rs.at[me], seq=target)

    for owner in range(owners):
        @pl.when(owner != me)
        def _():
            key_copy(owner).start()

    def gather(whole, send, recv, step):
        return remote(
            whole.at[me], whole.at[me], send.at[step], recv.at[me], seq=lax.rem(me + step, count)
        )

    def arrival(whole, send, recv, step):
        other = lax.rem(me + step, count)
        return remote(whole.at[other], whole.at[other], send.at[step], recv.at[other], seq=other)

    summed = q_own[...]
    for step in range(1, count):
        other = lax.rem(me + step, count)
        remote(q_loc.at[other], q_recv.at[other], r_ss.at[other], r_rs.at[other], seq=other).wait_recv()
        summed = summed + q_recv[other].astype(F32)
    q_all[me] = summed.astype(BF16)
    for step in range(1, count):
        gather(q_all, a_ss, a_rs, step).start()

    @pl.when(me < owners)
    def _():
        key_sum = k_loc[lax.rem(me, owners)]
        for step in range(1, count):
            other = lax.rem(me + step, count)
            remote(k_loc.at[0], k_recv.at[other], n_ss.at[0], n_rs.at[other], seq=other).wait_recv()
            key_sum = key_sum + k_recv[other]
        k_all[lax.rem(me, owners)] = key_sum
        for step in range(1, count):
            spot = lax.rem(me, owners)
            remote(k_all.at[spot], k_all.at[spot], m_ss.at[step], m_rs.at[spot], seq=lax.rem(me + step, count)).start()

    gk_ref[...] = product(key_dlog, kmap, NT)

    def to_queries(turn, carry):
        for h in range(batch):
            g = turn * batch + h
            place = pl.ds(pl.multiple_of(g * rows, rows), rows)
            gq_ref[:, pl.ds(pl.multiple_of(g * dim, dim), dim)] = product(
                split(dlog_s[place, :]), split(qmap_ref[g]), NT
            )
        return carry

    lax.fori_loop(0, group // batch, to_queries, 0)
    for store in stores[:3]:
        store.start()

    for owner in range(owners):
        @pl.when(owner != me)
        def _():
            remote(k_all.at[owner], k_all.at[owner], m_ss.at[0], m_rs.at[owner], seq=owner).wait_recv()
    k_sum = k_all[...].reshape(owners * k_shard, half)
    for step in range(1, count):
        arrival(q_all, a_ss, a_rs, step).wait_recv()
    q_sum = q_all[...].astype(F32).reshape(count * shard, half)
    squares = jnp.sum(q_sum * q_sum, axis=0, keepdims=True) + jnp.sum(k_sum * k_sum, axis=0, keepdims=True)
    squares = jnp.sum(squares, axis=1, keepdims=True)
    norm_all[my_head] = jnp.broadcast_to(squares, (8, dim))
    for step in range(1, heads):
        remote(
            norm_all.at[my_head], norm_all.at[my_head], h_ss.at[step], h_rs.at[my_head],
            head=lax.rem(my_head + step, heads),
        ).start()
    for step in range(1, heads):
        other = lax.rem(my_head + step, heads)
        remote(norm_all.at[other], norm_all.at[other], h_ss.at[step], h_rs.at[other], head=other).wait_recv()
    squared = norm_all[0][:1, :1]
    for other in range(1, heads):
        squared = squared + norm_all[other][:1, :1]
    limit = 0.25 * math.sqrt((group + 1) * heads * dim * half)
    factor = jnp.minimum(1.0, limit / (jnp.sqrt(squared) + EPSILON))
    gqm_ref[...] = factor * q_sum
    gkm_ref[...] = factor * k_sum
    for store in stores[3:]:
        store.start()

    for step in range(1, reach + 1):
        @pl.when(me + step < count)
        def _():
            for copy in block_copies(step):
                copy.wait_send()

        @pl.when(me >= step)
        def _():
            back_copy(step).wait_send()

    for step in range(1, count):
        shard_copy(lax.rem(me + step, count)).wait_send()
        gather(q_all, a_ss, a_rs, step).wait_send()

        @pl.when(me < owners)
        def _():
            spot = lax.rem(me, owners)
            remote(k_all.at[spot], k_all.at[spot], m_ss.at[step], m_rs.at[spot], seq=lax.rem(me + step, count)).wait_send()

    for owner in range(owners):
        @pl.when(owner != me)
        def _():
            key_copy(owner).wait_send()

    for step in range(1, heads):
        remote(
            norm_all.at[my_head], norm_all.at[my_head], h_ss.at[step], h_rs.at[my_head],
            head=lax.rem(my_head + step, heads),
        ).wait_send()
    for store in stores:
        store.wait()


def finish(*refs):
    size = (len(refs) - 2) // 3
    sources, targets, held = (refs[:size], refs[size : 2 * size], refs[2 * size : 3 * size])
    incoming = [pltpu.make_async_copy(sources[i], held[i], refs[-2].at[i]) for i in range(size)]
    outgoing = [pltpu.make_async_copy(held[i], targets[i], refs[-1].at[i]) for i in range(size)]
    for copy in incoming:
        copy.start()
    for copy, after in zip(incoming, outgoing):
        copy.wait()
        after.start()
    for copy in outgoing:
        copy.wait()


def on_device(queries, key_vectors, value_vectors, positions, query_map, key_map):
    count = lax.axis_size("seq")
    heads = lax.axis_size("head")
    rows, dim = key_vectors.shape
    group, _, half = query_map.shape
    feat = 2 * half
    reach = max(1, count // 2)
    batch = min(4, group)
    shard = group * dim // count
    total = group * rows
    k_shard = max(8, dim // count)
    owners = dim // k_shard
    hbm = pl.BlockSpec(memory_space=pltpu.HBM)
    dma = pltpu.SemaphoreType.DMA
    outs = pl.pallas_call(
        functools.partial(kernel, count, heads, reach, batch),
        out_shape=(
            jax.ShapeDtypeStruct((rows, group * dim), F32),
            jax.ShapeDtypeStruct((rows, dim), F32),
            jax.ShapeDtypeStruct((rows, dim), F32),
            jax.ShapeDtypeStruct((group * dim, half), F32),
            jax.ShapeDtypeStruct((dim, half), F32),
        ),
        in_specs=[hbm] * 6,
        out_specs=(hbm,) * 5,
        scratch_shapes=[
            pltpu.VMEM((rows, group * dim), BF16),
            pltpu.VMEM((1, rows), jnp.int32),
            pltpu.VMEM(query_map.shape, F32),
            pltpu.VMEM(key_map.shape, F32),
            dma((6,)),
            pltpu.VMEM((rows, group * dim), F32),
            pltpu.VMEM((rows, dim), F32),
            pltpu.VMEM((rows, dim), F32),
            pltpu.VMEM((group * dim, half), F32),
            pltpu.VMEM((dim, half), F32),
            dma((5,)),
            pltpu.VMEM(((reach + 1) * rows, dim), BF16),
            pltpu.VMEM(((reach + 1) * rows, dim), BF16),
            pltpu.VMEM((rows, (reach + 1) * rows), F32),
            pltpu.VMEM((total, feat), F32),
            pltpu.VMEM((total, rows), F32),
            pltpu.VMEM((total, dim), F32),
            pltpu.VMEM((total, dim), F32),
            pltpu.VMEM((total, half), F32),
            pltpu.VMEM((feat + 16, dim), F32),
            pltpu.VMEM((feat + 16, dim), BF16),
            pltpu.VMEM((reach, feat + 16, dim), BF16),
            pltpu.VMEM((count, shard, half), BF16),
            pltpu.VMEM((count, shard, half), BF16),
            pltpu.VMEM((count, shard, half), BF16),
            pltpu.VMEM((shard, half), F32),
            pltpu.VMEM((owners, k_shard, half), F32),
            pltpu.VMEM((count, k_shard, half), F32),
            pltpu.VMEM((owners, k_shard, half), F32),
            pltpu.VMEM((heads, 8, dim), F32),
            dma((reach,)), dma((reach,)), dma((reach,)), dma((reach,)), dma((reach,)), dma((reach,)),
            dma((count,)), dma((count,)), dma((count,)), dma((count,)), dma((count,)), dma((count,)),
            dma((count,)), dma((count,)), dma((heads,)), dma((heads,)),
        ],
        compiler_params=pltpu.CompilerParams(
            collective_id=0, has_side_effects=True, vmem_limit_bytes=GRANT
        ),
    )(queries, key_vectors, value_vectors, positions.reshape(1, rows), query_map, key_map)
    outs = pl.pallas_call(
        finish,
        out_shape=tuple(jax.ShapeDtypeStruct(out.shape, out.dtype) for out in outs),
        in_specs=[hbm] * 5,
        out_specs=(hbm,) * 5,
        scratch_shapes=[pltpu.VMEM(out.shape, out.dtype) for out in outs] + [dma((5,)), dma((5,))],
        compiler_params=pltpu.CompilerParams(vmem_limit_bytes=GRANT),
    )(*outs)
    return (
        outs[0], outs[1], outs[2],
        outs[3].reshape(group, dim, half), outs[4].reshape(1, dim, half),
    )


def solution(mesh):
    placed = (
        P("seq", "head"),
        P("seq", "head"),
        P("seq", "head"),
        P("seq"),
        P("head", None, None),
        P("head", None, None),
    )
    return jax.shard_map(
        on_device,
        mesh=mesh,
        in_specs=placed,
        out_specs=(
            P("seq", "head"),
            P("seq", "head"),
            P("seq", "head"),
            P("head", None, None),
            P("head", None, None),
        ),
        check_vma=False,
    )
```

profile of v0, /device:TPU:0, one launch (start us, length us, event | category | flops | bytes accessed | tf_op | source)
XLA Modules:
  0.0 53.0 jit_solution(4783545506409442794)
XLA Ops:
  0.6 50.2 %shard_map.101 = (f32[128,1024]{1,0:T(8,128)}, f32[128,128]{1,0:T(8,128)}, f32[128,128]{1,0:T(8,128)}, f32[1024,128]{1,0:T(8,128)}, f32[128,128]{1,0:T(8,128)}) custom-call(bf16[128,1024]{1,0:T(8,128)(2,1)} %q_hbm.1, bf16[128,128]{1,0:T(8,128)(2,1)} %k_hbm.1, bf16[128,128]{1,0:T(8,128)(2,1)} %v_hbm.1, s32[1,128]{1,0:T(1,128)} %bitcast.3, ...), custom_call_target="tpu_custom_call" | custom-call | tf_op jit(solution)/shard_map/pallas_call | solution.py:451
  50.8 2.1 %shard_map.102 = (f32[128,1024]{1,0:T(8,128)}, f32[128,128]{1,0:T(8,128)}, f32[128,128]{1,0:T(8,128)}, f32[1024,128]{1,0:T(8,128)}, f32[128,128]{1,0:T(8,128)}) custom-call(f32[128,1024]{1,0:T(8,128)} %get-tuple-element.15.refs_0_, f32[128,128]{1,0:T(8,128)} %get-tuple-element.16.refs_1_, f32[128,128]{1,0:T(8,128)} %get-tuple-element.17.refs_2_, ...), custom_call_target="tpu_custom_call" | custom-call | tf_op jit(solution)/shard_map/pallas_call | solution.py:501
where the time goes:
time: 53.1 us; the launch traced here: 53 us
  Pallas kernels  52.3 us (98%)
  between operations  0.64 us (1%)
    pallas_call x1, Pallas kernels, on_device(): pl.pallas_call(functools.partial(kernel, count, heads, reach, batch), out...  50.2 us
    pallas_call x1, Pallas kernels, on_device(): pl.pallas_call(finish, out_shape=tuple((jax.ShapeDtypeStruct(out.shape, o...  2.15 us

commit v1 on v0

--- a/solution.py
+++ b/solution.py
@@ -12,6 +12,7 @@
 BF16 = jnp.bfloat16
 NEGATIVE = -1e30
 EPSILON = 1e-06
+UNIT = 16
 GRANT = 66_000_000
 MESH = pl.DeviceIdType.MESH
 
@@ -61,16 +62,16 @@
     q_ref, pos_ref, qmap_ref, kmap_ref, load_s,
     gq_ref, gk_ref, gv_ref, gqm_ref, gkm_ref, store_s,
     win_k, win_v, bias, phi, inner_s, gn_s, gd_s, dlog_s, back_s, back_send, back_recv,
-    q_loc, q_recv, q_all, q_own, k_loc, k_recv, k_all, norm_all,
-    k_ss, k_rs, v_ss, v_rs, b_ss, b_rs, r_ss, r_rs, a_ss, a_rs, m_ss, m_rs, n_ss, n_rs, h_ss, h_rs,
+    past_s, q_loc, q_recv, q_all, q_own, k_loc, k_recv, k_all, norm_head, norm_seq,
+    k_ss, k_rs, v_ss, v_rs, b_ss, b_rs, r_ss, r_rs, a_ss, a_rs, m_ss, m_rs, n_ss, n_rs, h_ss, h_rs, w_ss, w_rs,
 ):
     me = lax.axis_index("seq")
     my_head = lax.axis_index("head")
     rows, dim = k_hbm.shape
     group, _, half = qmap_ref.shape
     feat = 2 * half
-    per_head = count // group
-    shard = dim // per_head
+    turns = group // batch
+    parts = dim // UNIT
     span = batch * rows
     scaling = 1.0 / math.sqrt(dim)
     k_shard = k_loc.shape[1]
@@ -91,6 +92,10 @@
             ((gq_ref, gq_hbm), (gk_ref, gk_hbm), (gv_ref, gv_hbm), (gqm_ref, gqm_hbm), (gkm_ref, gkm_hbm))
         )
     ]
+
+    def owner_slot(h, part):
+        unit = h * parts + part
+        return (unit % count, unit // count)
 
     def remote(src, dst, send, recv, **where):
         return pltpu.make_async_remote_copy(
@@ -174,6 +179,7 @@
     past_phi = softmax_pair(product((earlier,), kmap, NN))
     past_index = (me - reach) * rows + lax.broadcasted_iota(jnp.int32, (reach * rows, 1), 0)
     past_phi = past_phi * jnp.where(past_index >= first_start, 1.0, 0.0)
+    past_s[...] = past_phi
     state = product(split(past_phi), (win_v[: reach * rows, :],), TN)
     norms = jnp.sum(past_phi, axis=0, keepdims=True)
     state_parts = split(state)
@@ -187,10 +193,10 @@
         )
 
     def forward(turn):
-        place = pl.ds(pl.multiple_of(turn * span, span), span)
+        place = pl.ds(turn * span, span)
         q = jnp.concatenate(
             [
-                q_ref[:, pl.ds(pl.multiple_of((turn * batch + h) * dim, dim), dim)]
+                q_ref[:, (turn * batch + h) * dim : (turn * batch + h + 1) * dim]
                 for h in range(batch)
             ],
             axis=0,
@@ -222,12 +228,12 @@
         back_s[feat : feat + 1, :] += down[:, :half]
         back_s[feat + 1 : feat + 2, :] += down[:, half:]
 
-    def shard_copy(target):
-        return remote(q_loc.at[target], q_recv.at[me], r_ss.at[target], r_rs.at[me], seq=target)
+    def shard_copy(turn, target):
+        return remote(q_loc.at[turn, target], q_recv.at[turn, me], r_ss.at[turn], r_rs.at[turn], seq=target)
 
     def backward(turn, carry):
         grad_kphi, grad_values = carry
-        place = pl.ds(pl.multiple_of(turn * span, span), span)
+        place = pl.ds(turn * span, span)
         q_phi = phi[place, :]
         grad_numer = split(gn_s[place, :])
         grad_denom = gd_s[place, :1]
@@ -241,21 +247,15 @@
         dlog_s[place, :] = dlog
         for h in range(batch):
             g = turn * batch + h
-            q = q_ref[:, pl.ds(pl.multiple_of(g * dim, dim), dim)]
+            q = q_ref[:, g * dim : (g + 1) * dim]
             grad_map = product((q,), split(dlog[h * rows : (h + 1) * rows]), TN)
-            for part in range(per_head):
-                target = g * per_head + part
-                piece = grad_map[part * shard : (part + 1) * shard]
-                q_loc[target] = piece.astype(BF16)
-
-                @pl.when(target == me)
-                def _():
-                    q_own[...] = piece
-
-                @pl.when(target != me)
-                def _():
-                    shard_copy(target).start()
-
+            for part in range(parts):
+                owner, slot = owner_slot(h, part)
+                piece = grad_map[part * UNIT : (part + 1) * UNIT]
+                q_loc[turn, owner, slot * UNIT : (slot + 1) * UNIT, :] = piece.astype(BF16)
+                q_own[turn, owner, slot * UNIT : (slot + 1) * UNIT, :] = piece
+        for step in range(1, count):
+            shard_copy(turn, lax.rem(me + step, count)).start()
         grad_kphi = grad_kphi + product(mixing, split(q_phi), TN)
         grad_values = grad_values + product(split(inner_s[place, :]), grad_numer, TN)
         return (grad_kphi, grad_values)
@@ -267,20 +267,108 @@
         )
 
     sums = (jnp.zeros((rows, feat), F32), jnp.zeros((rows, dim), F32))
-    for turn in range(group // batch):
+    for turn in range(turns):
         forward(turn)
-        if turn == group // batch - 1:
-            origin = jnp.floor(first_start.astype(F32) * (1.0 / rows))
-            back_s[feat + 8 :, :] = jnp.broadcast_to(origin, (back_s.shape[0] - feat - 8, dim))
-            back_send[...] = back_s[...].astype(BF16)
-
-            for step in range(1, reach + 1):
-                @pl.when(me >= step)
-                def _():
-                    back_copy(step).start()
-
         sums = backward(turn, sums)
     grad_kphi, grad_values = sums
+
+    down_parts = split(back_s[:feat, :])
+    down_norms = jnp.concatenate([back_s[feat : feat + 1, :], back_s[feat + 1 : feat + 2, :]], axis=1)
+    past_grad = product((win_v[: reach * rows, :],), down_parts, NT) + down_norms
+    past_dlog = split(feature_back(past_s[...], past_grad, half))
+    own_dlog = split(feature_back(key_phi, grad_kphi, half))
+    key_grad = product((k_ref[...],), own_dlog, TN) + product((win_k[: reach * rows, :],), past_dlog, TN)
+    for owner in range(owners):
+        k_loc[owner] = key_grad[owner * k_shard : (owner + 1) * k_shard]
+
+    def key_copy(target):
+        return remote(k_loc.at[target], k_recv.at[me], n_ss.at[target], n_rs.at[me], seq=target)
+
+    for owner in range(owners):
+        @pl.when(owner != me)
+        def _():
+            key_copy(owner).start()
+
+    origin = jnp.floor(first_start.astype(F32) * (1.0 / rows))
+    back_s[feat + 8 :, :] = jnp.broadcast_to(origin, (back_s.shape[0] - feat - 8, dim))
+    back_send[...] = back_s[...].astype(BF16)
+
+    def gather(turn, step):
+        return remote(
+            q_all.at[turn, me], q_all.at[turn, me], a_ss.at[turn], a_rs.at[turn], seq=lax.rem(me + step, count)
+        )
+
+    def every(whole, turn, send, recv):
+        place = whole.at[turn, pl.ds(0, count - 1)]
+        return remote(place, place, send.at[turn], recv.at[turn], seq=lax.rem(me + 1, count))
+
+    def reduced(turn):
+        every(q_recv, turn, r_ss, r_rs).wait_recv()
+        summed = q_own[turn, me]
+        for step in range(1, count):
+            summed = summed + q_recv[turn, lax.rem(me + step, count)].astype(F32)
+        q_all[turn, me] = summed.astype(BF16)
+        for step in range(1, count):
+            gather(turn, step).start()
+        return jnp.sum(summed * summed, axis=0, keepdims=True)
+
+    squares = jnp.zeros((1, half), F32)
+    for turn in range(turns - 1):
+        squares = squares + reduced(turn)
+
+    for step in range(1, reach + 1):
+        @pl.when(me >= step)
+        def _():
+            back_copy(step).start()
+
+    def to_queries(turn, carry):
+        for h in range(batch):
+            g = turn * batch + h
+            place = pl.ds(pl.multiple_of(g * rows, rows), rows)
+            gq_ref[:, pl.ds(pl.multiple_of(g * dim, dim), dim)] = product(
+                split(dlog_s[place, :]), split(qmap_ref[g]), NT
+            )
+        return carry
+
+    lax.fori_loop(0, turns, to_queries, 0)
+    stores[0].start()
+
+    squares = squares + reduced(turns - 1)
+    norm_head[my_head] = squares
+
+    @pl.when(me < owners)
+    def _():
+        key_sum = k_loc[lax.rem(me, owners)]
+        for step in range(1, count):
+            other = lax.rem(me + step, count)
+            remote(k_loc.at[0], k_recv.at[other], n_ss.at[0], n_rs.at[other], seq=other).wait_recv()
+            key_sum = key_sum + k_recv[other]
+        k_all[lax.rem(me, owners)] = key_sum
+        norm_head[my_head] = squares + jnp.sum(key_sum * key_sum, axis=0, keepdims=True)
+
+    for step in range(1, heads):
+        remote(
+            norm_head.at[my_head], norm_head.at[my_head], h_ss.at[step], h_rs.at[my_head],
+            head=lax.rem(my_head + step, heads),
+        ).start()
+
+    @pl.when(me < owners)
+    def _():
+        for step in range(1, count):
+            spot = lax.rem(me, owners)
+            remote(k_all.at[spot], k_all.at[spot], m_ss.at[step], m_rs.at[spot], seq=lax.rem(me + step, count)).start()
+
+    for step in range(1, heads):
+        other = lax.rem(my_head + step, heads)
+        remote(norm_head.at[other], norm_head.at[other], h_ss.at[step], h_rs.at[other], head=other).wait_recv()
+    total_squares = norm_head[0]
+    for other in range(1, heads):
+        total_squares = total_squares + norm_head[other]
+    norm_seq[me] = total_squares
+    for step in range(1, count):
+        remote(
+            norm_seq.at[me], norm_seq.at[me], w_ss.at[step], w_rs.at[me], seq=lax.rem(me + step, count)
+        ).start()
 
     for step in range(1, reach + 1):
         @pl.when(me + step < count)
@@ -300,120 +388,68 @@
     back_parts = single(back[:feat])
     grad_kphi = grad_kphi + keeping * (product(value, back_parts, NT) + back_norms)
     gv_ref[...] = grad_values + keeping * product(key_parts, back_parts, NN)
-    key_dlog = split(feature_back(key_phi, grad_kphi, half))
-    key_grad = product((k_ref[...],), key_dlog, TN)
-    for owner in range(owners):
-        k_loc[owner] = key_grad[owner * k_shard : (owner + 1) * k_shard]
-
-    def key_copy(target):
-        return remote(k_loc.at[target], k_recv.at[me], n_ss.at[target], n_rs.at[me], seq=target)
-
+    gk_ref[...] = product(split(feature_back(key_phi, grad_kphi, half)), kmap, NT)
+    stores[1].start()
+    stores[2].start()
+
+    for step in range(1, count):
+        other = lax.rem(me + step, count)
+        remote(norm_seq.at[other], norm_seq.at[other], w_ss.at[step], w_rs.at[other], seq=other).wait_recv()
+    squares = norm_seq[0]
+    for other in range(1, count):
+        squares = squares + norm_seq[other]
+    squared = jnp.sum(squares, axis=1, keepdims=True)
+    limit = 0.25 * math.sqrt((group + 1) * heads * dim * half)
+    factor = jnp.minimum(1.0, limit / (jnp.sqrt(squared) + EPSILON))
+    for turn in range(turns):
+        every(q_all, turn, a_ss, a_rs).wait_recv()
+        for h in range(batch):
+            for part in range(parts):
+                owner, slot = owner_slot(h, part)
+                first = (turn * batch + h) * dim + part * UNIT
+                gqm_ref[first : first + UNIT, :] = factor * q_all[
+                    turn, owner, slot * UNIT : (slot + 1) * UNIT, :
+                ].astype(F32)
+    stores[3].start()
     for owner in range(owners):
         @pl.when(owner != me)
         def _():
-            key_copy(owner).start()
-
-    def gather(whole, send, recv, step):
-        return remote(
-            whole.at[me], whole.at[me], send.at[step], recv.at[me], seq=lax.rem(me + step, count)
-        )
-
-    def arrival(whole, send, recv, step):
-        other = lax.rem(me + step, count)
-        return remote(whole.at[other], whole.at[other], send.at[step], recv.at[other], seq=other)
-
-    summed = q_own[...]
+            remote(k_all.at[owner], k_all.at[owner], m_ss.at[0], m_rs.at[owner], seq=owner).wait_recv()
+    gkm_ref[...] = factor * k_all[...].reshape(owners * k_shard, half)
+    stores[4].start()
+
+    for step in range(1, reach + 1):
+        @pl.when(me + step < count)
+        def _():
+            for copy in block_copies(step):
+                copy.wait_send()
+
+        @pl.when(me >= step)
+        def _():
+            back_copy(step).wait_send()
+
+    for turn in range(turns):
+        every(q_loc, turn, r_ss, r_rs).wait_send()
+        every(q_all, turn, a_ss, a_rs).wait_send()
+
     for step in range(1, count):
-        other = lax.rem(me + step, count)
-        remote(q_loc.at[other], q_recv.at[other], r_ss.at[other], r_rs.at[other], seq=other).wait_recv()
-        summed = summed + q_recv[other].astype(F32)
-    q_all[me] = summed.astype(BF16)
-    for step in range(1, count):
-        gather(q_all, a_ss, a_rs, step).start()
-
-    @pl.when(me < owners)
-    def _():
-        key_sum = k_loc[lax.rem(me, owners)]
-        for step in range(1, count):
-            other = lax.rem(me + step, count)
-            remote(k_loc.at[0], k_recv.at[other], n_ss.at[0], n_rs.at[other], seq=other).wait_recv()
-            key_sum = key_sum + k_recv[other]
-        k_all[lax.rem(me, owners)] = key_sum
-        for step in range(1, count):
+        remote(
+            norm_seq.at[me], norm_seq.at[me], w_ss.at[step], w_rs.at[me], seq=lax.rem(me + step, count)
+        ).wait_send()
+
+        @pl.when(me < owners)
+        def _():
             spot = lax.rem(me, owners)
-            remote(k_all.at[spot], k_all.at[spot], m_ss.at[step], m_rs.at[spot], seq=lax.rem(me + step, count)).start()
-
-    gk_ref[...] = product(key_dlog, kmap, NT)
-
-    def to_queries(turn, carry):
-        for h in range(batch):
-            g = turn * batch + h
-            place = pl.ds(pl.multiple_of(g * rows, rows), rows)
-            gq_ref[:, pl.ds(pl.multiple_of(g * dim, dim), dim)] = product(
-                split(dlog_s[place, :]), split(qmap_ref[g]), NT
-            )
-        return carry
-
-    lax.fori_loop(0, group // batch, to_queries, 0)
-    for store in stores[:3]:
-        store.start()
+            remote(k_all.at[spot], k_all.at[spot], m_ss.at[step], m_rs.at[spot], seq=lax.rem(me + step, count)).wait_send()
 
     for owner in range(owners):
         @pl.when(owner != me)
         def _():
-            remote(k_all.at[owner], k_all.at[owner], m_ss.at[0], m_rs.at[owner], seq=owner).wait_recv()
-    k_sum = k_all[...].reshape(owners * k_shard, half)
-    for step in range(1, count):
-        arrival(q_all, a_ss, a_rs, step).wait_recv()
-    q_sum = q_all[...].astype(F32).reshape(count * shard, half)
-    squares = jnp.sum(q_sum * q_sum, axis=0, keepdims=True) + jnp.sum(k_sum * k_sum, axis=0, keepdims=True)
-    squares = jnp.sum(squares, axis=1, keepdims=True)
-    norm_all[my_head] = jnp.broadcast_to(squares, (8, dim))
+            key_copy(owner).wait_send()
+
     for step in range(1, heads):
         remote(
-            norm_all.at[my_head], norm_all.at[my_head], h_ss.at[step], h_rs.at[my_head],
-            head=lax.rem(my_head + step, heads),
-        ).start()
-    for step in range(1, heads):
-        other = lax.rem(my_head + step, heads)
-        remote(norm_all.at[other], norm_all.at[other], h_ss.at[step], h_rs.at[other], head=other).wait_recv()
-    squared = norm_all[0][:1, :1]
-    for other in range(1, heads):
-        squared = squared + norm_all[other][:1, :1]
-    limit = 0.25 * math.sqrt((group + 1) * heads * dim * half)
-    factor = jnp.minimum(1.0, limit / (jnp.sqrt(squared) + EPSILON))
-    gqm_ref[...] = factor * q_sum
-    gkm_ref[...] = factor * k_sum
-    for store in stores[3:]:
-        store.start()
-
-    for step in range(1, reach + 1):
-        @pl.when(me + step < count)
-        def _():
-            for copy in block_copies(step):
-                copy.wait_send()
-
-        @pl.when(me >= step)
-        def _():
-            back_copy(step).wait_send()
-
-    for step in range(1, count):
-        shard_copy(lax.rem(me + step, count)).wait_send()
-        gather(q_all, a_ss, a_rs, step).wait_send()
-
-        @pl.when(me < owners)
-        def _():
-            spot = lax.rem(me, owners)
-            remote(k_all.at[spot], k_all.at[spot], m_ss.at[step], m_rs.at[spot], seq=lax.rem(me + step, count)).wait_send()
-
-    for owner in range(owners):
-        @pl.when(owner != me)
-        def _():
-            key_copy(owner).wait_send()
-
-    for step in range(1, heads):
-        remote(
-            norm_all.at[my_head], norm_all.at[my_head], h_ss.at[step], h_rs.at[my_head],
+            norm_head.at[my_head], norm_head.at[my_head], h_ss.at[step], h_rs.at[my_head],
             head=lax.rem(my_head + step, heads),
         ).wait_send()
     for store in stores:
@@ -441,8 +477,9 @@
     group, _, half = query_map.shape
     feat = 2 * half
     reach = max(1, count // 2)
-    batch = min(4, group)
-    shard = group * dim // count
+    batch = min(group, max(2, UNIT * count // dim))
+    turns = group // batch
+    shard = batch * dim // count
     total = group * rows
     k_shard = max(8, dim // count)
     owners = dim // k_shard
@@ -482,17 +519,19 @@
             pltpu.VMEM((feat + 16, dim), F32),
             pltpu.VMEM((feat + 16, dim), BF16),
             pltpu.VMEM((reach, feat + 16, dim), BF16),
-            pltpu.VMEM((count, shard, half), BF16),
-            pltpu.VMEM((count, shard, half), BF16),
-            pltpu.VMEM((count, shard, half), BF16),
-            pltpu.VMEM((shard, half), F32),
+            pltpu.VMEM((reach * rows, feat), F32),
+            pltpu.VMEM((turns, count, shard, half), BF16),
+            pltpu.VMEM((turns, count, shard, half), BF16),
+            pltpu.VMEM((turns, count, shard, half), BF16),
+            pltpu.VMEM((turns, count, shard, half), F32),
             pltpu.VMEM((owners, k_shard, half), F32),
             pltpu.VMEM((count, k_shard, half), F32),
             pltpu.VMEM((owners, k_shard, half), F32),
-            pltpu.VMEM((heads, 8, dim), F32),
+            pltpu.VMEM((heads, 1, half), F32),
+            pltpu.VMEM((count, 1, half), F32),
             dma((reach,)), dma((reach,)), dma((reach,)), dma((reach,)), dma((reach,)), dma((reach,)),
-            dma((count,)), dma((count,)), dma((count,)), dma((count,)), dma((count,)), dma((count,)),
-            dma((count,)), dma((count,)), dma((heads,)), dma((heads,)),
+            dma((turns,)), dma((turns,)), dma((turns,)), dma((turns,)), dma((count,)), dma((count,)),
+            dma((count,)), dma((count,)), dma((heads,)), dma((heads,)), dma((count,)), dma((count,)),
         ],
         compiler_params=pltpu.CompilerParams(
             collective_id=0, has_side_effects=True, vmem_limit_bytes=GRANT

time: 53.1 us -> 46.7 us (0.88)
  Pallas kernels: 52.3 us -> 45.9 us
    pallas_call x1, Pallas kernels: 50.2 us -> 43.8 us  [on_device(): pl.pallas_call(functools.partial(kernel, count, heads, reach, batch), out...]
where the time goes in v1:
time: 46.7 us; the launch traced here: 46.5 us
  Pallas kernels  45.9 us (98%)
  between operations  0.64 us (1%)
    pallas_call x1, Pallas kernels, on_device(): pl.pallas_call(functools.partial(kernel, count, heads, reach, batch), out...  43.8 us
    pallas_call x1, Pallas kernels, on_device(): pl.pallas_call(finish, out_shape=tuple((jax.ShapeDtypeStruct(out.shape, o...  2.15 us

profile of v1, /device:TPU:0, one launch (start us, length us, event | category | flops | bytes accessed | tf_op | source)
XLA Modules:
  0.0 46.5 jit_solution(7953034447505866977)
XLA Ops:
  0.6 43.8 %shard_map.101 = (f32[128,1024]{1,0:T(8,128)}, f32[128,128]{1,0:T(8,128)}, f32[128,128]{1,0:T(8,128)}, f32[1024,128]{1,0:T(8,128)}, f32[128,128]{1,0:T(8,128)}) custom-call(bf16[128,1024]{1,0:T(8,128)(2,1)} %q_hbm.1, bf16[128,128]{1,0:T(8,128)(2,1)} %k_hbm.1, bf16[128,128]{1,0:T(8,128)(2,1)} %v_hbm.1, s32[1,128]{1,0:T(1,128)} %bitcast.3, ...), custom_call_target="tpu_custom_call" | custom-call | tf_op jit(solution)/shard_map/pallas_call | solution.py:488
  44.4 2.1 %shard_map.102 = (f32[128,1024]{1,0:T(8,128)}, f32[128,128]{1,0:T(8,128)}, f32[128,128]{1,0:T(8,128)}, f32[1024,128]{1,0:T(8,128)}, f32[128,128]{1,0:T(8,128)}) custom-call(f32[128,1024]{1,0:T(8,128)} %get-tuple-element.15.refs_0_, f32[128,128]{1,0:T(8,128)} %get-tuple-element.16.refs_1_, f32[128,128]{1,0:T(8,128)} %get-tuple-element.17.refs_2_, ...), custom_call_target="tpu_custom_call" | custom-call | tf_op jit(solution)/shard_map/pallas_call | solution.py:540
